TPU v7x, 512 devices: a whole 4x4x16 slice. The times are simulated.
512 devices in a mesh: shard: 128 (over y, z, core), tensor: 4 (over x).
Axes of the slice: x: 4, y: 4, z: 16, core: 2. Of those that a mesh axis runs over, the one named last changes fastest.
Arguments:
- expert_grads: bfloat16 [2, 128, 2, 512, 1024], P(None, 'shard', None, None, 'tensor')
- embed_grads: bfloat16 [2, 128, 4096, 512], P(None, 'shard', None, 'tensor')
- small_grads: bfloat16 [2, 128, 512, 36], P(None, 'shard', None, 'tensor')
- expert_master: float32 [2, 512, 1024], P(None, 'shard', 'tensor'), may hold values from -0.2 to 0.2
- expert_first: float32 [2, 512, 1024], P(None, 'shard', 'tensor'), may hold values from -6 to 6
- expert_second: float32 [2, 512, 1024], P(None, 'shard', 'tensor'), may hold values from 0.02 to 0.2
- embed_master: float32 [4096, 512], P('shard', 'tensor'), may hold values from -0.2 to 0.2
- embed_first: float32 [4096, 512], P('shard', 'tensor'), may hold values from -6 to 6
- embed_second: float32 [4096, 512], P('shard', 'tensor'), may hold values from 0.02 to 0.2
- small_master: float32 [512, 36], P('shard', 'tensor'), may hold values from -0.2 to 0.2
- small_first: float32 [512, 36], P('shard', 'tensor'), may hold values from -6 to 6
- small_second: float32 [512, 36], P('shard', 'tensor'), may hold values from 0.02 to 0.2
- class_steps: int32 [4096], P('shard'), may hold values from 1 to 2000
- clip_rms: float32 [], replicated, may hold values from 1 to 1.5
Outputs:
- expert_weights: bfloat16 [2, 512, 1024], P(None, None, 'tensor')
- embed_weights: bfloat16 [4096, 512], P(None, 'tensor')
- small_weights: bfloat16 [512, 36], P(None, 'tensor')
- expert_master_new: float32 [2, 512, 1024], P(None, 'shard', 'tensor')
- expert_first_new: float32 [2, 512, 1024], P(None, 'shard', 'tensor')
- expert_second_new: float32 [2, 512, 1024], P(None, 'shard', 'tensor')
- embed_master_new: float32 [4096, 512], P('shard', 'tensor')
- embed_first_new: float32 [4096, 512], P('shard', 'tensor')
- embed_second_new: float32 [4096, 512], P('shard', 'tensor')
- embed_step: float32 [4096, 512], P('shard', 'tensor')
- small_master_new: float32 [512, 36], P('shard', 'tensor')
- small_first_new: float32 [512, 36], P('shard', 'tensor')
- small_second_new: float32 [512, 36], P('shard', 'tensor')
- clip_scale: float32 [], replicated
All inputs are finite; a program needn't handle non-finite values.
Results may differ from a plain program's by a relative error of at most 0.001.
Values may be sent and summed in bfloat16 or wider, within the bound.
No kernel may reach another device: no remote copies, remote signals or barrier semaphores. Data moves between devices by JAX's collectives and lax.ppermute only.
A program may use at most 64 MiB of HBM per device.

v0:
```python
import jax
import jax.numpy as jnp
from jax import lax
from jax.sharding import PartitionSpec as P

STEP = 1000
P_TOT = 3164160
BETA_ONE = 0.9
BETA_TWO = 0.999
LEARN_RATE = 0.001
DECAY_RATE = 0.1
EPSILON = 1e-08


def local_total(gradients):
    summed = gradients[0, 0].astype(jnp.float32)
    summed = summed + gradients[1, 0].astype(jnp.float32)
    return summed


def finish(first_new, second_new, master, corr_one, corr_two):
    update_step = (
        first_new / corr_one / (jnp.sqrt(second_new / corr_two) + EPSILON) + DECAY_RATE * master
    )
    master_new = master - LEARN_RATE * update_step
    return (master_new, update_step)


def body(
    expert_grads,
    embed_grads,
    small_grads,
    expert_master,
    expert_first,
    expert_second,
    embed_master,
    embed_first,
    embed_second,
    small_master,
    small_first,
    small_second,
    class_steps,
    clip_rms,
):
    expert_local = local_total(expert_grads)
    embed_local = local_total(embed_grads)
    small_local = local_total(small_grads)
    expert_sum = lax.psum_scatter(expert_local, "shard", scatter_dimension=1, tiled=True)
    embed_sum = lax.psum_scatter(embed_local, "shard", scatter_dimension=0, tiled=True)
    small_sum = lax.psum_scatter(small_local, "shard", scatter_dimension=0, tiled=True)
    summed_all = (expert_sum, embed_sum, small_sum)
    squares = (
        jnp.sum(expert_sum * expert_sum)
        + jnp.sum(embed_sum * embed_sum)
        + jnp.sum(small_sum * small_sum)
    )
    total_squares = lax.psum(squares, ("shard", "tensor"))
    clip_factor = clip_rms * jnp.sqrt(P_TOT / total_squares)

    def moments(group_index, first_moment, second_moment):
        scaled = clip_factor * summed_all[group_index]
        return (
            BETA_ONE * first_moment + (1.0 - BETA_ONE) * scaled,
            BETA_TWO * second_moment + (1.0 - BETA_TWO) * scaled * scaled,
        )

    fixed_one = 1.0 - BETA_ONE**STEP
    fixed_two = 1.0 - BETA_TWO**STEP
    row_float = class_steps.astype(jnp.float32)[:, None]
    row_one = 1.0 - BETA_ONE**row_float
    row_two = 1.0 - BETA_TWO**row_float
    expert_first_new, expert_second_new = moments(0, expert_first, expert_second)
    embed_first_new, embed_second_new = moments(1, embed_first, embed_second)
    small_first_new, small_second_new = moments(2, small_first, small_second)
    expert_master_new, expert_update = finish(
        expert_first_new, expert_second_new, expert_master, fixed_one, fixed_two
    )
    embed_master_new, embed_update = finish(
        embed_first_new, embed_second_new, embed_master, row_one, row_two
    )
    small_master_new, small_update = finish(
        small_first_new, small_second_new, small_master, fixed_one, fixed_two
    )
    expert_cast = expert_master_new.astype(jnp.bfloat16)
    embed_cast = embed_master_new.astype(jnp.bfloat16)
    small_cast = small_master_new.astype(jnp.bfloat16)
    expert_weights = lax.all_gather(expert_cast, "shard", axis=1, tiled=True)
    embed_weights = lax.all_gather(embed_cast, "shard", axis=0, tiled=True)
    small_weights = lax.all_gather(small_cast, "shard", axis=0, tiled=True)
    return (
        expert_weights,
        embed_weights,
        small_weights,
        expert_master_new,
        expert_first_new,
        expert_second_new,
        embed_master_new,
        embed_first_new,
        embed_second_new,
        embed_update,
        small_master_new,
        small_first_new,
        small_second_new,
        clip_factor,
    )


def solution(mesh):
    in_specs = (
        P(None, "shard", None, None, "tensor"),
        P(None, "shard", None, "tensor"),
        P(None, "shard", None, "tensor"),
        P(None, "shard", "tensor"),
        P(None, "shard", "tensor"),
        P(None, "shard", "tensor"),
        P("shard", "tensor"),
        P("shard", "tensor"),
        P("shard", "tensor"),
        P("shard", "tensor"),
        P("shard", "tensor"),
        P("shard", "tensor"),
        P("shard"),
        P(),
    )
    out_specs = (
        P(None, None, "tensor"),
        P(None, "tensor"),
        P(None, "tensor"),
        P(None, "shard", "tensor"),
        P(None, "shard", "tensor"),
        P(None, "shard", "tensor"),
        P("shard", "tensor"),
        P("shard", "tensor"),
        P("shard", "tensor"),
        P("shard", "tensor"),
        P("shard", "tensor"),
        P("shard", "tensor"),
        P("shard", "tensor"),
        P(),
    )
    return jax.shard_map(body, mesh=mesh, in_specs=in_specs, out_specs=out_specs, check_vma=False)
```

profile of v0, /device:TPU:1, one launch (start us, length us, event | category | flops | bytes accessed | tf_op | source)
XLA Modules:
  0.0 900.7 jit_solution(16309437702115690155)
XLA Ops:
  7.2 0.0 copy-start
  7.2 0.0 all-reduce.4.cloned.1.call-start
  7.2 2.4 add_bitcast_fusion.1
  9.7 0.0 all-reduce.4.cloned.1.call-update
  9.7 0.0 reduce-scatter.3.cloned.1.call-start
  9.7 0.0 copy-done
  9.7 1.5 add_bitcast_fusion
  11.3 0.0 copy-start.1
  11.3 0.0 copy-start.11
  11.3 0.0 copy-start.2
  11.3 0.0 copy-start.3
  11.3 0.0 copy-start.4
  11.3 0.0 copy-start.5
  11.3 0.0 copy-start.6
  11.3 0.0 copy-start.7
  11.3 0.0 copy-start.8
  11.4 0.0 copy-start.9
  11.4 0.0 copy-start.10
  11.4 0.0 reduce-scatter.3.cloned.1.call-update
  11.4 0.0 all-gather.3.cloned.1.call-start
  11.5 0.5 copy-done.1
  12.1 0.1 copy.38
  12.2 1.3 dynamic-slice
  14.1 498.3 %all-reduce.1 = f32[512,9]{1,0:T(8,128)S(1)} all-reduce(f32[512,9]{1,0:T(8,128)S(1)} %copy.38), channel_id=4, replica_groups=mesh['shard'=128,'tensor'=4] {'shard'}, use_global_device_ids=true, to_apply=%region_4.0.clone | all-reduce | flops 4608 | bytes 36864
  512.4 0.6 multiply_reduce_fusion.2
  513.0 0.0 copy-done.11
  513.0 0.0 all-reduce.4.cloned.1.call-done
  513.1 1.3 multiply_reduce_fusion.1
  514.4 91.1 %reduce-scatter.3.cloned.1.call-done = f32[32,128]{1,0:T(8,128)} async-done(((f32[4096,128]{1,0:T(8,128)}), f32[32,128]{1,0:T(8,128)}) %reduce-scatter.3.cloned.1.call-update) | async-done | bytes 16400 | tf_op jit(solution)/shard_map/reduce_scatter | solution.py:49
  605.5 1.3 multiply_reduce_fusion
  609.4 112.9 %psum.7 = f32[]{:T(128)} all-reduce(f32[]{:T(128)S(6)} %add.84), channel_id=1, replica_groups=mesh['shard'=128,'tensor'=4] {'shard','tensor'}, use_global_device_ids=true, to_apply=%region_6.0 | all-reduce | flops 1 | bytes 8 | tf_op jit(solution)/shard_map/psum | solution.py:57
  723.0 0.0 copy-done.2
  723.0 0.0 copy-done.3
  723.0 0.0 copy-done.4
  723.0 1.4 fusion.4
  724.5 0.0 all-gather.3.cloned.1.call-update
  724.5 0.0 copy-done.5
  724.5 0.0 copy-done.6
  724.5 0.0 copy-done.7
  724.5 1.4 fusion.6
  725.9 81.5 %all_gather.9 = bf16[2,512,256]{2,0,1:T(2,128)(2,1)S(1)} all-gather(bf16[2,4,256]{2,0,1:T(2,128)(2,1)S(1)} %copy.39), channel_id=1, replica_groups=mesh['shard'=128,'tensor'=4] {'shard'}, dimensions={1}, use_global_device_ids=true | all-gather | bytes 528384 | tf_op jit(solution)/shard_map/all_gather | solution.py:87
  807.4 0.9 copy.40
  808.2 0.0 copy-done.8
  808.2 0.0 copy-done.9
  808.2 0.0 copy-done.10
  808.2 0.6 convert_bitcast_fusion
  808.8 81.2 %all-gather = bf16[128,4,9]{2,1,0:T(4,128)(2,1)S(1)} all-gather(bf16[1,4,9]{2,1,0:T(4,128)(2,1)S(1)} %get-tuple-element.56), channel_id=1, replica_groups=mesh['shard'=128,'tensor'=4] {'shard'}, dimensions={0}, use_global_device_ids=true | all-gather | bytes 9288 | tf_op jit(solution)/shard_map/all_gather | solution.py:89
  890.1 0.7 copy.41
  890.8 0.0 all-gather.3.cloned.1.call-done
  890.8 2.3 copy.51
  (4 shorter events, 0.0 us)
Async XLA Ops:
  7.2 2.6 copy-start
  7.2 505.9 %all-reduce.4.cloned.1.call-start = ((), (), s32[]{:S(2)}) async-start(), calls=%async_computation.3 | async-start | bytes 2097152
  9.7 595.8 %reduce-scatter.3.cloned.1.call-start = ((), (), s32[]{:S(2)}) async-start(), calls=%async_computation.1 | async-start | bytes 2113536 | tf_op jit(solution)/shard_map/reduce_scatter | solution.py:49
  11.3 0.7 copy-start.1
  11.3 501.7 %copy-start.11 = (s32[32]{0:T(128)S(1)}, s32[32]{0:T(128)}, u32[]{:S(2)}) copy-start(s32[32]{0:T(128)} %param.26) | copy-start | bytes 388
  11.3 711.7 %copy-start.2 = (f32[32,128]{1,0:T(8,128)S(1)}, f32[32,128]{1,0:T(8,128)}, u32[]{:S(2)}) copy-start(f32[32,128]{1,0:T(8,128)} %param.20) | copy-start | bytes 49156
  11.3 711.7 %copy-start.3 = (f32[32,128]{1,0:T(8,128)S(1)}, f32[32,128]{1,0:T(8,128)}, u32[]{:S(2)}) copy-start(f32[32,128]{1,0:T(8,128)} %param.22) | copy-start | bytes 49156
  11.3 711.7 %copy-start.4 = (f32[32,128]{1,0:T(8,128)S(1)}, f32[32,128]{1,0:T(8,128)}, u32[]{:S(2)}) copy-start(f32[32,128]{1,0:T(8,128)} %param.21) | copy-start | bytes 49156
  11.3 713.2 %copy-start.5 = (f32[2,4,256]{2,1,0:T(4,128)S(1)}, f32[2,4,256]{2,1,0:T(4,128)}, u32[]{:S(2)}) copy-start(f32[2,4,256]{2,1,0:T(4,128)} %param.17) | copy-start | bytes 24580
  11.3 713.2 %copy-start.6 = (f32[2,4,256]{2,1,0:T(4,128)S(1)}, f32[2,4,256]{2,1,0:T(4,128)}, u32[]{:S(2)}) copy-start(f32[2,4,256]{2,1,0:T(4,128)} %param.19) | copy-start | bytes 24580
  11.3 713.2 %copy-start.7 = (f32[2,4,256]{2,1,0:T(4,128)S(1)}, f32[2,4,256]{2,1,0:T(4,128)}, u32[]{:S(2)}) copy-start(f32[2,4,256]{2,1,0:T(4,128)} %param.18) | copy-start | bytes 24580
  11.3 796.9 %copy-start.8 = (f32[4,9]{1,0:T(4,128)S(1)}, f32[4,9]{1,0:T(4,128)}, u32[]{:S(2)}) copy-start(f32[4,9]{1,0:T(4,128)} %param.23) | copy-start | bytes 436
  11.4 796.9 %copy-start.9 = (f32[4,9]{1,0:T(4,128)S(1)}, f32[4,9]{1,0:T(4,128)}, u32[]{:S(2)}) copy-start(f32[4,9]{1,0:T(4,128)} %param.25) | copy-start | bytes 436
  11.4 796.9 %copy-start.10 = (f32[4,9]{1,0:T(4,128)S(1)}, f32[4,9]{1,0:T(4,128)}, u32[]{:S(2)}) copy-start(f32[4,9]{1,0:T(4,128)} %param.24) | copy-start | bytes 436
  11.4 879.4 %all-gather.3.cloned.1.call-start = ((), (), s32[]{:S(2)}) async-start(), calls=%async_computation.2 | async-start | bytes 1056768 | tf_op jit(solution)/shard_map/all_gather | solution.py:88
Sparse Core Ops, SparseCore 0:
  12.1 340.1 all-reduce.3
  357.5 247.9 reduce-scatter.2
  724.6 125.6 all-gather.2
where the time goes:
time: 901 us
  blocking collectives  774 us (86%)
  waiting for transfers between devices  91.2 us (10%)
  between operations  19 us (2%)
  other arithmetic  10.6 us (1%)
    unnamed x1, blocking collectives  498 us
    psum x1, blocking collectives, body(): total_squares = lax.psum(squares, ('shard', 'tensor'))  113 us
    reduce_scatter x1, waiting for transfers between devices, body(): lax.psum_scatter(embed_local, 'shard', scatter_dimension=0, tiled=True)  91.1 us
    all_gather x1, blocking collectives, body(): expert_weights = lax.all_gather(expert_cast, 'shard', axis=1, tiled=True)  81.5 us
    all_gather x1, blocking collectives, body(): small_weights = lax.all_gather(small_cast, 'shard', axis=0, tiled=True)  81.2 us
  transfers between devices with their start and end apart: 3, of which 1 were waited for; matrix products, arithmetic and copies ran while one was open for 1% of the time, Pallas kernels for 0%

commit v1 on v0

--- a/solution.py
+++ b/solution.py
@@ -86,7 +86,9 @@
     small_cast = small_master_new.astype(jnp.bfloat16)
     expert_weights = lax.all_gather(expert_cast, "shard", axis=1, tiled=True)
     embed_weights = lax.all_gather(embed_cast, "shard", axis=0, tiled=True)
-    small_weights = lax.all_gather(small_cast, "shard", axis=0, tiled=True)
+    small_weights = jnp.concatenate(
+        lax.all_to_all(jnp.stack([small_cast] * lax.axis_size("shard")), "shard", 0, 0), axis=0
+    )
     return (
         expert_weights,
         embed_weights,

time: 901 us -> 861 us (0.956)
  blocking collectives: 774 us -> 696 us
  waiting for transfers between devices: 91.2 us -> 117 us
  starting transfers between devices: 0.12 us -> 11.3 us
    all_gather x1 -> x0, blocking collectives: 81.2 us -> none  [body(): small_weights = lax.all_gather(small_cast, 'shard', axis=0, tiled=True)]
    all_gather x1, waiting for transfers between devices: 0.01 us -> 25.8 us  [body(): embed_weights = lax.all_gather(embed_cast, 'shard', axis=0, tiled=True)]
    all_to_all x0 -> x1, starting transfers between devices: none -> 11.2 us  [body(): lax.all_to_all(jnp.stack([small_cast] * lax.axis_size('shard')), 'shard',...]
  transfers between devices with their start and end apart: 3 -> 4, of which waited for: 1 -> 2; matrix products, arithmetic and copies ran while one was open for 1% -> 1% of each run, Pallas kernels for 0% -> 0%
where the time goes in v1:
time: 861 us
  blocking collectives  696 us (81%)
  waiting for transfers between devices  117 us (14%)
  between operations  19.1 us (2%)
  starting transfers between devices  11.3 us (1%)
  other arithmetic  10.7 us (1%)
    unnamed x1, blocking collectives  498 us
    psum x1, blocking collectives, body(): total_squares = lax.psum(squares, ('shard', 'tensor'))  113 us
    reduce_scatter x1, waiting for transfers between devices, body(): lax.psum_scatter(embed_local, 'shard', scatter_dimension=0, tiled=True)  91.1 us
    all_gather x1, blocking collectives, body(): expert_weights = lax.all_gather(expert_cast, 'shard', axis=1, tiled=True)  84.9 us
    all_gather x1, waiting for transfers between devices, body(): embed_weights = lax.all_gather(embed_cast, 'shard', axis=0, tiled=True)  25.8 us
  transfers between devices with their start and end apart: 4, of which 2 were waited for; matrix products, arithmetic and copies ran while one was open for 1% of the time, Pallas kernels for 0%

profile of v1, /device:TPU:1, one launch (start us, length us, event | category | flops | bytes accessed | tf_op | source)
XLA Modules:
  0.0 860.7 jit_solution(17718128355158944314)
XLA Ops:
  7.2 0.0 copy-start
  7.2 0.0 all-reduce.4.cloned.1.call-start
  7.2 2.4 add_bitcast_fusion.1
  9.7 0.0 all-reduce.4.cloned.1.call-update
  9.7 0.0 reduce-scatter.3.cloned.1.call-start
  9.7 0.0 copy-done
  9.7 1.6 add_bitcast_fusion
  11.3 0.0 copy-start.1
  11.3 0.0 copy-start.11
  11.3 0.0 copy-start.2
  11.3 0.0 copy-start.3
  11.3 0.0 copy-start.4
  11.3 0.0 copy-start.5
  11.3 0.0 copy-start.6
  11.3 0.0 copy-start.7
  11.4 0.0 copy-start.8
  11.4 0.0 copy-start.9
  11.4 0.0 copy-start.10
  11.4 0.0 reduce-scatter.3.cloned.1.call-update
  11.4 0.0 all-gather.2.cloned.1.call-start
  11.5 0.5 copy-done.1
  12.1 0.1 copy.41
  12.2 1.3 dynamic-slice
  14.1 498.2 %all-reduce.1 = f32[512,9]{1,0:T(8,128)S(1)} all-reduce(f32[512,9]{1,0:T(8,128)S(1)} %copy.41), channel_id=4, replica_groups=mesh['shard'=128,'tensor'=4] {'shard'}, use_global_device_ids=true, to_apply=%region_4.0.clone | all-reduce | flops 4608 | bytes 36864
  512.4 0.6 multiply_reduce_fusion.2
  513.0 0.0 copy-done.11
  513.0 0.0 all-reduce.4.cloned.1.call-done
  513.0 1.3 multiply_reduce_fusion.1
  514.4 91.1 %reduce-scatter.3.cloned.1.call-done = f32[32,128]{1,0:T(8,128)} async-done(((f32[4096,128]{1,0:T(8,128)}), f32[32,128]{1,0:T(8,128)}) %reduce-scatter.3.cloned.1.call-update) | async-done | bytes 16400 | tf_op jit(solution)/shard_map/reduce_scatter | solution.py:49
  605.5 1.3 multiply_reduce_fusion
  609.4 112.9 %psum.7 = f32[]{:T(128)} all-reduce(f32[]{:T(128)S(6)} %add.84), channel_id=1, replica_groups=mesh['shard'=128,'tensor'=4] {'shard','tensor'}, use_global_device_ids=true, to_apply=%region_6.0 | all-reduce | flops 1 | bytes 8 | tf_op jit(solution)/shard_map/psum | solution.py:57
  723.0 0.0 copy-done.2
  723.0 0.0 copy-done.3
  723.1 0.0 copy-done.4
  723.1 1.4 fusion.5
  724.5 0.0 all-gather.2.cloned.1.call-update
  724.5 0.0 copy-done.5
  724.5 0.0 copy-done.6
  724.5 0.0 copy-done.7
  724.6 1.4 fusion.7
  725.9 0.0 copy-done.8
  725.9 0.0 copy-done.9
  725.9 0.0 copy-done.10
  725.9 0.6 fusion.3
  726.6 0.7 stack.2
  727.2 11.2 %all-to-all-start = ((bf16[128,4,9]{2,1,0:T(4,128)(2,1)}), bf16[128,4,9]{2,1,0:T(4,128)(2,1)S(1)}, u32[]{:S(2)}, u32[]{:S(2)}) async-start(bf16[128,4,9]{2,1,0:T(4,128)(2,1)} %stack.2), calls=%async_computation.1 | async-start | bytes 262144 | tf_op jit(solution)/shard_map/all_to_all | solution.py:90
  738.5 84.9 %all_gather.6 = bf16[2,512,256]{2,0,1:T(2,128)(2,1)S(1)} all-gather(bf16[2,4,256]{2,0,1:T(2,128)(2,1)S(1)} %copy.42), channel_id=1, replica_groups=mesh['shard'=128,'tensor'=4] {'shard'}, dimensions={1}, use_global_device_ids=true | all-gather | bytes 528384 | tf_op jit(solution)/shard_map/all_gather | solution.py:87
  823.4 0.9 copy.43
  824.3 0.0 all-to-all-done
  824.3 0.7 copy.44
  825.0 25.8 %all-gather.2.cloned.1.call-done = bf16[4096,128]{1,0:T(8,128)(2,1)} async-done(((bf16[32,128]{1,0:T(8,128)(2,1)}), bf16[4096,128]{1,0:T(8,128)(2,1)}) %all-gather.2.cloned.1.call-update) | async-done | bytes 1048592 | tf_op jit(solution)/shard_map/all_gather | solution.py:88
  850.8 2.3 copy.54
  (4 shorter events, 0.0 us)
Async XLA Ops:
  7.2 2.6 copy-start
  7.2 505.8 %all-reduce.4.cloned.1.call-start = ((), (), s32[]{:S(2)}) async-start(), calls=%async_computation.4 | async-start | bytes 2097152
  9.7 595.8 %reduce-scatter.3.cloned.1.call-start = ((), (), s32[]{:S(2)}) async-start(), calls=%async_computation.2 | async-start | bytes 2113536 | tf_op jit(solution)/shard_map/reduce_scatter | solution.py:49
  11.3 0.7 copy-start.1
  11.3 501.7 %copy-start.11 = (s32[32]{0:T(128)S(1)}, s32[32]{0:T(128)}, u32[]{:S(2)}) copy-start(s32[32]{0:T(128)} %param.26) | copy-start | bytes 388
  11.3 711.7 %copy-start.2 = (f32[32,128]{1,0:T(8,128)S(1)}, f32[32,128]{1,0:T(8,128)}, u32[]{:S(2)}) copy-start(f32[32,128]{1,0:T(8,128)} %param.20) | copy-start | bytes 49156
  11.3 711.7 %copy-start.3 = (f32[32,128]{1,0:T(8,128)S(1)}, f32[32,128]{1,0:T(8,128)}, u32[]{:S(2)}) copy-start(f32[32,128]{1,0:T(8,128)} %param.22) | copy-start | bytes 49156
  11.3 711.8 %copy-start.4 = (f32[32,128]{1,0:T(8,128)S(1)}, f32[32,128]{1,0:T(8,128)}, u32[]{:S(2)}) copy-start(f32[32,128]{1,0:T(8,128)} %param.21) | copy-start | bytes 49156
  11.3 713.2 %copy-start.5 = (f32[2,4,256]{2,1,0:T(4,128)S(1)}, f32[2,4,256]{2,1,0:T(4,128)}, u32[]{:S(2)}) copy-start(f32[2,4,256]{2,1,0:T(4,128)} %param.17) | copy-start | bytes 24580
  11.3 713.2 %copy-start.6 = (f32[2,4,256]{2,1,0:T(4,128)S(1)}, f32[2,4,256]{2,1,0:T(4,128)}, u32[]{:S(2)}) copy-start(f32[2,4,256]{2,1,0:T(4,128)} %param.19) | copy-start | bytes 24580
  11.3 713.2 %copy-start.7 = (f32[2,4,256]{2,1,0:T(4,128)S(1)}, f32[2,4,256]{2,1,0:T(4,128)}, u32[]{:S(2)}) copy-start(f32[2,4,256]{2,1,0:T(4,128)} %param.18) | copy-start | bytes 24580
  11.4 714.6 %copy-start.8 = (f32[4,9]{1,0:T(4,128)S(1)}, f32[4,9]{1,0:T(4,128)}, u32[]{:S(2)}) copy-start(f32[4,9]{1,0:T(4,128)} %param.23) | copy-start | bytes 436
  11.4 714.6 %copy-start.9 = (f32[4,9]{1,0:T(4,128)S(1)}, f32[4,9]{1,0:T(4,128)}, u32[]{:S(2)}) copy-start(f32[4,9]{1,0:T(4,128)} %param.25) | copy-start | bytes 436
  11.4 714.6 %copy-start.10 = (f32[4,9]{1,0:T(4,128)S(1)}, f32[4,9]{1,0:T(4,128)}, u32[]{:S(2)}) copy-start(f32[4,9]{1,0:T(4,128)} %param.24) | copy-start | bytes 436
  11.4 839.3 %all-gather.2.cloned.1.call-start = ((), (), s32[]{:S(2)}) async-start(), calls=%async_computation.3 | async-start | bytes 1056768 | tf_op jit(solution)/shard_map/all_gather | solution.py:88
  727.2 97.0 %all-to-all-start = ((bf16[128,4,9]{2,1,0:T(4,128)(2,1)}), bf16[128,4,9]{2,1,0:T(4,128)(2,1)S(1)}, u32[]{:S(2)}, u32[]{:S(2)}) async-start(bf16[128,4,9]{2,1,0:T(4,128)(2,1)} %stack.2), calls=%async_computation.1 | async-start | bytes 262144 | tf_op jit(solution)/shard_map/all_to_all | solution.py:90
Sparse Core Ops, SparseCore 0:
  12.1 340.0 all-reduce.3
  357.5 247.9 reduce-scatter.2
  724.6 126.0 all-gather.1
